TPU v7x, 512 devices: a whole 4x4x16 slice. The times are simulated.
512 devices in a mesh: blk: 128 (over y_hi, z, x), feat: 4 (over y_lo, core).
Axes of the slice: x: 4, y: 4 (y_hi: 2, y_lo: 2; y = y_hi * 2 + y_lo), z: 16, core: 2. Of those that a mesh axis runs over, the one named last changes fastest.
Arguments:
- features: bfloat16 [256, 131072], P('feat', 'blk'), may hold values from -6 to 6
- block_values: bfloat16 [17408, 128, 128], P('blk'), may hold values from 0 to 1, as said below
- block_rows: int32 [17408], P('blk'), may hold values from 0 to 7, as said below
- block_cols: int32 [17408], P('blk'), may hold values from 0 to 1023, as said below
- block_count: int32 [128], P('blk'), may hold values from 8 to 136, as said below
- labels: int32 [131072], P(('blk', 'feat')), may hold values from 0 to 127
- weight_in: bfloat16 [256, 256], replicated, may hold values from -0.375 to 0.375
- weight_out: bfloat16 [256, 128], replicated, may hold values from -1 to 1
Outputs:
- logits: float32 [128, 131072], P(None, ('blk', 'feat'))
- grad_in: float32 [256, 256], replicated
- grad_out: float32 [256, 128], replicated
Inputs may be any that keep to these rules, and one draw needn't show every extreme that they name: The first block_count[s] slots of stripe s are its blocks; the remaining slots hold blocks that are not part of the matrix; every stripe holds its 8 diagonal blocks, and the busiest stripe fills all 136 slots. `block_rows`: block row of a slot inside its stripe. `block_cols`: every slot's block column lies within 8 blocks of its global block row, counted around the loop of 1024 block columns; the live slots of a stripe name distinct blocks. `block_values`: the matrix assembled from the live slots is symmetric: live block (r, c) is the transpose of live block (c, r).
All inputs are finite; a program needn't handle non-finite values.
Results may differ from a plain program's by a relative error of at most 0.002.
The roundings to bfloat16 on the way count: a program that leaves them out, or rounds other values in their place, can miss the bound.
Values may be sent and summed in bfloat16 or wider, within the bound.
No kernel may reach another device: no remote copies, remote signals or barrier semaphores. Data moves between devices by JAX's collectives and lax.ppermute only.
A program may use at most 64 MiB of HBM per device.

v0:
```python
import math
import jax
import jax.numpy as jnp
from jax import lax
from jax.sharding import PartitionSpec as P


def extended_2(cells, sides, width):
    for axis, dim in sides:
        count = lax.axis_size(axis)
        head = lax.slice_in_dim(cells, 0, width, axis=dim)
        tail = lax.slice_in_dim(cells, cells.shape[dim] - width, cells.shape[dim], axis=dim)
        cells = jnp.concatenate(
            [
                lax.ppermute(tail, axis, [(i, (i + 1) % count) for i in range(count)]),
                cells,
                lax.ppermute(head, axis, [((i + 1) % count, i) for i in range(count)]),
            ],
            axis=dim,
        )
    return cells


def propagate(extended, block_values, local_index, placing, precise):
    channels = extended.shape[0]
    block_size = block_values.shape[1]
    blocked = extended.reshape(channels, extended.shape[1] // block_size, block_size)
    gathered = jnp.take(blocked, local_index, axis=1)
    if precise:
        products = jnp.einsum(
            "csb,sab->csa",
            gathered,
            block_values.astype(jnp.float32),
            precision=lax.Precision.HIGHEST,
        )
    else:
        products = jnp.einsum(
            "csb,sab->csa", gathered, block_values, preferred_element_type=jnp.float32
        )
    placed = jnp.einsum("csa,sr->cra", products, placing, precision=lax.Precision.HIGHEST)
    return placed.reshape(channels, placing.shape[1] * block_size)


def activation(entry_value):
    return jax.nn.gelu(entry_value, approximate=True)


def on_device(
    features, block_values, block_rows, block_cols, block_count, labels, weight_in, weight_out
):
    device_count = lax.axis_size("blk")
    stripe_index = lax.axis_index("blk")
    block_size = block_values.shape[1]
    slot_count = block_rows.shape[0]
    stripe_rows = features.shape[1]
    stripe_blocks = stripe_rows // block_size
    reach_blocks = (slot_count // stripe_blocks - 1) // 2
    total_blocks = stripe_blocks * device_count
    local_index = jnp.mod(block_cols - (stripe_index * stripe_blocks - reach_blocks), total_blocks)
    live_slots = jnp.arange(slot_count, dtype=jnp.int32) < block_count[0]
    placing = (
        (block_rows[:, None] == jnp.arange(stripe_blocks, dtype=jnp.int32)[None, :])
        & live_slots[:, None]
    ).astype(jnp.float32)
    band_width = reach_blocks * block_size
    node_scale = 1.0 / math.sqrt(device_count * stripe_rows)
    input_ext = extended_2(features, (("blk", 1),), band_width)
    prop_in = propagate(input_ext, block_values, local_index, placing, False).astype(jnp.bfloat16)
    prop_rows_in = lax.all_to_all(prop_in, "feat", split_axis=1, concat_axis=0, tiled=True)
    pre_hidden = jnp.einsum(
        "ih,ir->hr", weight_in, prop_rows_in, preferred_element_type=jnp.float32
    )
    hidden = activation(pre_hidden).astype(jnp.bfloat16)
    hidden_cols = lax.all_to_all(hidden, "feat", split_axis=0, concat_axis=1, tiled=True)
    hidden_ext = extended_2(hidden_cols, (("blk", 1),), band_width)
    prop_hid = propagate(hidden_ext, block_values, local_index, placing, False).astype(jnp.bfloat16)
    prop_rows_hid = lax.all_to_all(prop_hid, "feat", split_axis=1, concat_axis=0, tiled=True)
    logits = jnp.einsum("hc,hr->cr", weight_out, prop_rows_hid, preferred_element_type=jnp.float32)
    class_count = weight_out.shape[1]
    shifted = logits - jnp.max(logits, axis=0, keepdims=True)
    exponent = jnp.exp(shifted)
    probability = exponent / jnp.sum(exponent, axis=0, keepdims=True)
    onehot = (labels[None, :] == jnp.arange(class_count, dtype=jnp.int32)[:, None]).astype(
        jnp.float32
    )
    dlogits = ((probability - onehot) * node_scale).astype(jnp.bfloat16)
    out_share = jnp.einsum("hr,cr->hc", prop_rows_hid, dlogits, preferred_element_type=jnp.float32)
    grad_out = lax.psum(out_share, ("blk", "feat"))
    back_rows = jnp.einsum("hc,cr->hr", weight_out, dlogits, preferred_element_type=jnp.float32)
    back_cols = lax.all_to_all(
        back_rows.astype(jnp.bfloat16), "feat", split_axis=0, concat_axis=1, tiled=True
    ).astype(back_rows.dtype)
    back_ext = extended_2(back_cols.astype(jnp.bfloat16), (("blk", 1),), band_width).astype(
        back_cols.dtype
    )
    back_prop = propagate(back_ext, block_values, local_index, placing, True)
    back_hid = lax.all_to_all(
        back_prop.astype(jnp.bfloat16), "feat", split_axis=1, concat_axis=0, tiled=True
    ).astype(back_prop.dtype)
    unused_output, pullback = jax.vjp(activation, pre_hidden)
    grad_pre = pullback(back_hid)[0].astype(jnp.bfloat16)
    in_share = jnp.einsum("ir,hr->ih", prop_rows_in, grad_pre, preferred_element_type=jnp.float32)
    grad_in = lax.psum(in_share, ("blk", "feat"))
    return (logits, grad_in, grad_out)


def solution(mesh):
    placed = (
        P("feat", "blk"),
        P("blk", None, None),
        P("blk"),
        P("blk"),
        P("blk"),
        P(("blk", "feat")),
        P(),
        P(),
    )
    return jax.shard_map(
        on_device,
        mesh=mesh,
        in_specs=placed,
        out_specs=(P(None, ("blk", "feat")), P(), P()),
        check_vma=False,
    )
```

profile of v0, /device:TPU:2, one launch (start us, length us, event | category | flops | bytes accessed | tf_op | source)
XLA Modules:
  0.0 618.4 jit_solution(3650204196831870399)
XLA Ops:
  7.2 0.0 copy-start
  7.2 3.5 collective-permute-start
  10.7 6.3 %collective-permute-start.1 = (bf16[64,1024]{1,0:T(8,128)(2,1)}, bf16[64,1024]{1,0:T(8,128)(2,1)S(1)}, u32[]{:S(2)}, u32[]{:S(2)}) collective-permute-start(bf16[64,1024]{1,0:T(8,128)(2,1)} %param.10), channel_id=1, source_target_pairs={{4,0},{8,4},{12,8},{16,12},{20,16},{24,20},{28,24},{32,28},{36,32}... | collective-permute-start | bytes 393224 | tf_op jit(solution)/shard_map/ppermute | solution.py:17
  17.7 0.7 compare_and_fusion
  18.4 0.0 collective-permute-done
  18.4 1.4 collective-permute-done.1
  19.9 1.0 copy_bitcast_fusion
  20.9 1.0 gather_fusion.1
  21.9 0.0 copy-start.3
  21.9 5.4 fusion.19
  27.2 0.0 copy-done.3
  27.3 4.0 fusion.43
  31.3 0.1 convert_element_type.67
  31.4 7.0 %all_to_all.80 = bf16[64,4,256]{2,0,1:T(8,128)(2,1)S(1)} all-to-all(bf16[64,4,256]{2,0,1:T(8,128)(2,1)S(1)} %copy.36), channel_id=1, replica_groups=mesh['blk'=128,'feat'=4] {'feat'}, dimensions={1} | all-to-all | bytes 262144 | tf_op jit(solution)/shard_map/all_to_all | solution.py:69
  38.4 0.0 copy-done
  38.4 0.3 multiply_convert_fusion
  38.7 7.0 %all_to_all.81 = bf16[4,64,256]{2,1,0:T(8,128)(2,1)S(1)} all-to-all(bf16[4,64,256]{2,1,0:T(8,128)(2,1)S(1)} %bitcast.120), channel_id=1, replica_groups=mesh['blk'=128,'feat'=4] {'feat'}, dimensions={0} | all-to-all | bytes 262144 | tf_op jit(solution)/shard_map/all_to_all | solution.py:74
  45.7 11.1 %collective-permute-start.3 = (bf16[64,1024]{1,0:T(8,128)(2,1)S(1)}, bf16[64,1024]{1,0:T(8,128)(2,1)S(1)}, u32[]{:S(2)}, u32[]{:S(2)}) collective-permute-start(bf16[64,1024]{1,0:T(8,128)(2,1)S(1)} %bitcast.116), channel_id=1, source_target_pairs={{4,0},{8,4},{12,8},{16,12},{20,16},{24,20},{28,24},{32,28},{36,32}... | collective-permute-start | bytes 393224 | tf_op jit(solution)/shard_map/ppermute | solution.py:17
  56.8 2.1 collective-permute-start.2
  58.9 0.1 copy.37
  59.0 0.1 concatenate.25
  59.1 0.2 collective-permute-done.3
  59.3 10.4 %collective-permute-done.2 = bf16[64,1024]{1,0:T(8,128)(2,1)S(1)} collective-permute-done((bf16[64,1024]{1,0:T(8,128)(2,1)S(1)}, bf16[64,1024]{1,0:T(8,128)(2,1)S(1)}, u32[]{:S(2)}, u32[]{:S(2)}) %collective-permute-start.2) | collective-permute-done | bytes 131104 | tf_op jit(solution)/shard_map/ppermute | solution.py:15
  69.8 1.0 gather_fusion.2
  70.8 5.4 fusion.22
  76.2 0.0 copy-start.2
  76.2 0.0 copy-start.4
  76.2 4.0 fusion.40
  80.3 0.1 convert_element_type.71
  80.4 7.0 %all_to_all.82 = bf16[64,4,256]{2,0,1:T(8,128)(2,1)S(1)} all-to-all(bf16[64,4,256]{2,0,1:T(8,128)(2,1)S(1)} %copy.43), channel_id=1, replica_groups=mesh['blk'=128,'feat'=4] {'feat'}, dimensions={1} | all-to-all | bytes 262144 | tf_op jit(solution)/shard_map/all_to_all | solution.py:77
  87.4 0.0 copy-done.2
  87.4 0.2 fusion.75
  87.6 0.0 copy-start.1
  87.7 0.0 copy-done.4
  87.7 0.2 convolution_convert_fusion
  87.9 7.0 %all_to_all.83 = bf16[4,64,256]{2,1,0:T(8,128)(2,1)S(1)} all-to-all(bf16[4,64,256]{2,1,0:T(8,128)(2,1)S(1)} %bitcast.121), channel_id=1, replica_groups=mesh['blk'=128,'feat'=4] {'feat'}, dimensions={0} | all-to-all | bytes 262144 | tf_op jit(solution)/shard_map/all_to_all | solution.py:90
  94.9 9.6 %collective-permute-start.5 = (bf16[64,1024]{1,0:T(8,128)(2,1)S(1)}, bf16[64,1024]{1,0:T(8,128)(2,1)S(1)}, u32[]{:S(2)}, u32[]{:S(2)}) collective-permute-start(bf16[64,1024]{1,0:T(8,128)(2,1)S(1)} %bitcast.118), channel_id=1, source_target_pairs={{4,0},{8,4},{12,8},{16,12},{20,16},{24,20},{28,24},{32,28},{36,32}... | collective-permute-start | bytes 393224 | tf_op jit(solution)/shard_map/ppermute | solution.py:17
  104.5 2.1 collective-permute-start.4
  106.7 0.1 copy.44
  106.8 0.1 concatenate.29
  106.9 0.1 collective-permute-done.5
  107.1 4.3 collective-permute-done.4
  111.4 0.1 maximum_convert_fusion
  111.5 2.9 gather_fusion
  114.4 11.1 %fusion.25 = f32[64,136,128]{2,0,1:T(8,128)S(1)} fusion(bf16[136,128,128]{2,1,0:T(8,128)(2,1)} %param.11, f32[136,64,128]{2,1,0:T(8,128)} %gather_fusion, pred[136]{0:T(512)(128)(4,1)S(1)} %get-tuple-element.6), kind=kOutput, calls=%fused_computation.24 | convolution fusion | flops 1712390144 | bytes 13369480 | tf_op jit(solution)/shard_map/csb,sab->csa/dot_general | solution.py:30
  125.4 4.0 fusion.37
  129.5 0.1 convert_element_type.79
  129.6 0.7 copy.50
  130.2 3.3 all-to-all-start.4
  133.6 0.0 all-reduce.3.cloned.1.call-start
  133.6 0.0 copy-done.1
  133.6 0.9 fusion.74
  134.5 3.7 all-to-all-done.4
  138.1 0.2 fusion.54
  138.3 0.9 fusion.76
  139.3 0.0 all-reduce.3.cloned.1.call-update
  139.3 469.0 %all-reduce.3.cloned.1.call-done = (f32[256,256]{1,0:T(8,128)}, f32[256,128]{1,0:T(8,128)}) async-done(((f32[256,256]{1,0:T(8,128)}, f32[256,128]{1,0:T(8,128)}), (f32[256,256]{1,0:T(8,128)}, f32[256,128]{1,0:T(8,128)})) %all-reduce.3.cloned.1.call-update) | async-done | bytes 393232 | tf_op jit(solution)/shard_map/psum | solution.py:103
  608.3 1.7 copy.84
  610.0 1.6 copy.85
  (14 shorter events, 0.3 us)
Async XLA Ops:
  7.2 31.2 %copy-start = (bf16[256,256]{1,0:T(8,128)(2,1)S(1)}, bf16[256,256]{1,0:T(8,128)(2,1)}, u32[]{:S(2)}) copy-start(bf16[256,256]{1,0:T(8,128)(2,1)} %param.16) | copy-start | bytes 393220
  7.2 11.2 %collective-permute-start = (bf16[64,1024]{1,0:T(8,128)(2,1)}, bf16[64,1024]{1,0:T(8,128)(2,1)S(1)}, u32[]{:S(2)}, u32[]{:S(2)}) collective-permute-start(bf16[64,1024]{1,0:T(8,128)(2,1)} %param.10), channel_id=1, source_target_pairs={{0,4},{4,8},{8,12},{12,16},{16,20},{20,24},{24,28},{28,32},{32,36}... | collective-permute-start | bytes 393224 | tf_op jit(solution)/shard_map/ppermute | solution.py:15
  10.7 9.1 %collective-permute-start.1 = (bf16[64,1024]{1,0:T(8,128)(2,1)}, bf16[64,1024]{1,0:T(8,128)(2,1)S(1)}, u32[]{:S(2)}, u32[]{:S(2)}) collective-permute-start(bf16[64,1024]{1,0:T(8,128)(2,1)} %param.10), channel_id=1, source_target_pairs={{4,0},{8,4},{12,8},{16,12},{20,16},{24,20},{28,24},{32,28},{36,32}... | collective-permute-start | bytes 393224 | tf_op jit(solution)/shard_map/ppermute | solution.py:17
  21.9 5.4 copy-start.3
  45.7 13.6 %collective-permute-start.3 = (bf16[64,1024]{1,0:T(8,128)(2,1)S(1)}, bf16[64,1024]{1,0:T(8,128)(2,1)S(1)}, u32[]{:S(2)}, u32[]{:S(2)}) collective-permute-start(bf16[64,1024]{1,0:T(8,128)(2,1)S(1)} %bitcast.116), channel_id=1, source_target_pairs={{4,0},{8,4},{12,8},{16,12},{20,16},{24,20},{28,24},{32,28},{36,32}... | collective-permute-start | bytes 393224 | tf_op jit(solution)/shard_map/ppermute | solution.py:17
  56.8 12.9 %collective-permute-start.2 = (bf16[64,1024]{1,0:T(8,128)(2,1)S(1)}, bf16[64,1024]{1,0:T(8,128)(2,1)S(1)}, u32[]{:S(2)}, u32[]{:S(2)}) collective-permute-start(bf16[64,1024]{1,0:T(8,128)(2,1)S(1)} %bitcast.117), channel_id=1, source_target_pairs={{0,4},{4,8},{8,12},{12,16},{16,20},{20,24},{24,28},{28,32},{32,36}... | collective-permute-start | bytes 393224 | tf_op jit(solution)/shard_map/ppermute | solution.py:15
  76.2 11.2 %copy-start.2 = (bf16[256,128]{1,0:T(8,128)(2,1)S(1)}, bf16[256,128]{1,0:T(8,128)(2,1)}, u32[]{:S(2)}) copy-start(bf16[256,128]{1,0:T(8,128)(2,1)} %param.17) | copy-start | bytes 196612
  76.2 11.5 %copy-start.4 = (s32[256]{0:T(256)S(1)}, s32[256]{0:T(256)}, u32[]{:S(2)}) copy-start(s32[256]{0:T(256)} %param.15) | copy-start | bytes 3076
  87.6 46.0 %copy-start.1 = (f32[256,128]{0,1:T(8,128)}, f32[256,128]{0,1:T(8,128)S(1)}, u32[]{:S(2)}) copy-start(f32[256,128]{0,1:T(8,128)S(1)} %get-tuple-element.11) | copy-start | bytes 393220
  94.9 12.2 %collective-permute-start.5 = (bf16[64,1024]{1,0:T(8,128)(2,1)S(1)}, bf16[64,1024]{1,0:T(8,128)(2,1)S(1)}, u32[]{:S(2)}, u32[]{:S(2)}) collective-permute-start(bf16[64,1024]{1,0:T(8,128)(2,1)S(1)} %bitcast.118), channel_id=1, source_target_pairs={{4,0},{8,4},{12,8},{16,12},{20,16},{24,20},{28,24},{32,28},{36,32}... | collective-permute-start | bytes 393224 | tf_op jit(solution)/shard_map/ppermute | solution.py:17
  104.5 6.9 %collective-permute-start.4 = (bf16[64,1024]{1,0:T(8,128)(2,1)S(1)}, bf16[64,1024]{1,0:T(8,128)(2,1)S(1)}, u32[]{:S(2)}, u32[]{:S(2)}) collective-permute-start(bf16[64,1024]{1,0:T(8,128)(2,1)S(1)} %bitcast.119), channel_id=1, source_target_pairs={{0,4},{4,8},{8,12},{12,16},{16,20},{20,24},{24,28},{28,32},{32,36}... | collective-permute-start | bytes 393224 | tf_op jit(solution)/shard_map/ppermute | solution.py:15
  130.2 7.9 %all-to-all-start.4 = ((bf16[64,4,256]{2,0,1:T(8,128)(2,1)}), bf16[64,4,256]{2,0,1:T(8,128)(2,1)S(1)}, u32[]{:S(2)}, u32[]{:S(2)}) async-start(bf16[64,4,256]{2,0,1:T(8,128)(2,1)} %copy.50), calls=%async_computation.4 | async-start | bytes 262144 | tf_op jit(solution)/shard_map/all_to_all | solution.py:97
  133.6 474.8 %all-reduce.3.cloned.1.call-start = ((), (), s32[]{:S(2)}) async-start(), calls=%async_computation.5 | async-start | bytes 786432 | tf_op jit(solution)/shard_map/psum | solution.py:103
Sparse Core Ops, SparseCore 0:
  140.4 467.8 all-reduce.2
where the time goes:
time: 619 us; the launch traced here: 618 us
  waiting for transfers between devices  489 us (79%)
  starting transfers between devices  38.2 us (6%)
  matrix products  36.4 us (6%)
  blocking collectives  28 us (5%)
  between operations  15 us (2%)
  local copies, waits for them, and re-layouts  9.57 us (2%)
    psum x1, waiting for transfers between devices, on_device(): grad_in = lax.psum(in_share, ('blk', 'feat'))  469 us
    ppermute x3, starting transfers between devices, extended_2(): lax.ppermute(head, axis, [((i + 1) % count, i) for i in range(count)])  27.1 us
    ppermute x3, waiting for transfers between devices, extended_2(): lax.ppermute(tail, axis, [(i, (i + 1) % count) for i in range(count)])  14.8 us
  transfers between devices with their start and end apart: 8, of which 7 were waited for; matrix products, arithmetic and copies ran while one was open for 0% of the time, Pallas kernels for 0%

commit v1 on v0

--- a/solution.py
+++ b/solution.py
@@ -100,7 +100,7 @@
     unused_output, pullback = jax.vjp(activation, pre_hidden)
     grad_pre = pullback(back_hid)[0].astype(jnp.bfloat16)
     in_share = jnp.einsum("ir,hr->ih", prop_rows_in, grad_pre, preferred_element_type=jnp.float32)
-    grad_in = lax.psum(in_share, ("blk", "feat"))
+    grad_in = lax.psum(lax.psum(in_share, "blk"), "feat")
     return (logits, grad_in, grad_out)
 
 

time: 619 us -> 1870 us (3.02)
  the two profiles are of different devices: /device:TPU:2 before, /device:TPU:1 now
where the time goes in v1:
time: 1870 us
  waiting for transfers between devices  1730 us (93%)
  blocking collectives  38 us (2%)
  matrix products  36.4 us (2%)
  starting transfers between devices  36.1 us (2%)
    psum x2, waiting for transfers between devices, on_device(): grad_in = lax.psum(lax.psum(in_share, 'blk'), 'feat')  1220 us
    psum x1, waiting for transfers between devices, on_device(): grad_out = lax.psum(out_share, ('blk', 'feat'))  491 us
  transfers between devices with their start and end apart: 9, of which 7 were waited for; matrix products, arithmetic and copies ran while one was open for 0% of the time, Pallas kernels for 0%

profile of v1, /device:TPU:1, one launch (start us, length us, event | category | flops | bytes accessed | tf_op | source)
XLA Modules:
  0.0 1866.4 jit_solution(16552248980187968288)
XLA Ops:
  7.2 0.0 copy-start
  7.2 0.0 all-reduce.4.cloned.1.call-start
  7.2 3.9 collective-permute-start
  11.2 14.8 collective-permute-start.1
  26.6 0.7 compare_and_fusion
  27.3 0.1 collective-permute-done
  27.4 1.0 collective-permute-done.1
  28.4 1.0 copy_bitcast_fusion
  29.4 1.0 gather_fusion.1
  30.4 0.0 copy-start.3
  30.4 5.4 fusion.19
  35.8 0.0 copy-done.3
  35.8 4.0 fusion.43
  39.8 0.1 convert_element_type.67
  40.0 7.5 all_to_all.80
  47.4 0.0 copy-done
  47.4 0.3 multiply_convert_fusion
  47.7 7.0 all_to_all.81
  54.7 9.7 collective-permute-start.3
  64.5 2.1 collective-permute-start.2
  66.6 0.1 copy.37
  66.7 0.1 concatenate.25
  66.8 0.0 collective-permute-done.3
  66.8 9.1 collective-permute-done.2
  76.0 1.0 gather_fusion.2
  77.0 5.4 fusion.22
  82.3 0.0 copy-start.2
  82.4 0.0 copy-start.4
  82.4 4.0 fusion.40
  86.4 0.1 convert_element_type.71
  86.5 8.4 all_to_all.82
  94.9 0.0 copy-done.2
  94.9 0.2 fusion.75
  95.2 0.0 copy-start.1
  95.2 0.0 copy-done.4
  95.2 0.2 convolution_convert_fusion
  95.4 7.0 all_to_all.83
  102.4 1.9 collective-permute-start.5
  104.4 3.6 collective-permute-start.4
  108.0 0.1 copy.44
  108.1 0.1 concatenate.29
  108.2 0.0 collective-permute-done.5
  108.2 7.6 collective-permute-done.4
  115.8 0.1 maximum_convert_fusion
  115.9 2.9 gather_fusion
  118.8 11.1 fusion.25
  129.9 4.0 fusion.37
  133.9 0.1 convert_element_type.79
  134.0 8.1 all_to_all.84
  142.1 0.2 fusion.54
  142.3 0.9 fusion.76
  143.3 0.0 all-reduce.4.cloned.1.call-update
  143.3 0.0 all-reduce.8.cloned.1.call-start
  143.3 0.0 copy-done.1
  143.4 0.9 fusion.74
  144.2 0.0 all-reduce.8.cloned.1.call-update
  144.2 0.0 all-reduce.6.cloned.1.call-start
  144.3 1175.7 %all-reduce.4.cloned.1.call-done = f32[256,256]{1,0:T(8,128)} async-done(((f32[256,256]{1,0:T(8,128)}), f32[256,256]{1,0:T(8,128)}) %all-reduce.4.cloned.1.call-update) | async-done | bytes 262160 | tf_op jit(solution)/shard_map/psum | solution.py:103
  1320.0 0.0 all-reduce.6.cloned.1.call-update
  1320.1 491.3 %all-reduce.8.cloned.1.call-done = f32[256,128]{1,0:T(8,128)} async-done(((f32[256,128]{1,0:T(8,128)}), f32[256,128]{1,0:T(8,128)}) %all-reduce.8.cloned.1.call-update) | async-done | bytes 131088 | tf_op jit(solution)/shard_map/psum | solution.py:88
  1811.4 45.2 %all-reduce.6.cloned.1.call-done = f32[256,256]{1,0:T(8,128)} async-done(((f32[256,256]{1,0:T(8,128)}), f32[256,256]{1,0:T(8,128)}) %all-reduce.6.cloned.1.call-update) | async-done | bytes 262160 | tf_op jit(solution)/shard_map/psum | solution.py:103
  1856.6 1.7 copy.85
  1858.3 1.6 copy.86
  (15 shorter events, 0.3 us)
Async XLA Ops:
  7.2 40.3 %copy-start = (bf16[256,256]{1,0:T(8,128)(2,1)S(1)}, bf16[256,256]{1,0:T(8,128)(2,1)}, u32[]{:S(2)}) copy-start(bf16[256,256]{1,0:T(8,128)(2,1)} %param.16) | copy-start | bytes 393220
  7.2 1312.9 %all-reduce.4.cloned.1.call-start = ((), (), s32[]{:S(2)}) async-start(), calls=%async_computation.5 | async-start | bytes 524288 | tf_op jit(solution)/shard_map/psum | solution.py:103
  7.2 20.2 %collective-permute-start = (bf16[64,1024]{1,0:T(8,128)(2,1)}, bf16[64,1024]{1,0:T(8,128)(2,1)S(1)}, u32[]{:S(2)}, u32[]{:S(2)}) collective-permute-start(bf16[64,1024]{1,0:T(8,128)(2,1)} %param.10), channel_id=1, source_target_pairs={{0,4},{4,8},{8,12},{12,16},{16,20},{20,24},{24,28},{28,32},{32,36}... | collective-permute-start | bytes 393224 | tf_op jit(solution)/shard_map/ppermute | solution.py:15
  11.2 17.2 collective-permute-start.1
  30.4 5.4 copy-start.3
  54.7 12.1 collective-permute-start.3
  64.5 11.4 collective-permute-start.2
  82.3 12.6 copy-start.2
  82.4 12.9 copy-start.4
  95.2 48.2 %copy-start.1 = (f32[256,128]{0,1:T(8,128)}, f32[256,128]{0,1:T(8,128)S(1)}, u32[]{:S(2)}) copy-start(f32[256,128]{0,1:T(8,128)S(1)} %get-tuple-element.9) | copy-start | bytes 393220
  102.4 5.7 collective-permute-start.5
  104.4 11.4 collective-permute-start.4
  143.3 1668.1 %all-reduce.8.cloned.1.call-start = ((), (), s32[]{:S(2)}) async-start(), calls=%async_computation.7 | async-start | bytes 262144 | tf_op jit(solution)/shard_map/psum | solution.py:88
  144.2 1712.4 %all-reduce.6.cloned.1.call-start = ((), (), s32[]{:S(2)}) async-start(), calls=%async_computation.6 | async-start | bytes 524288 | tf_op jit(solution)/shard_map/psum | solution.py:103
Sparse Core Ops, SparseCore 0:
  143.4 1176.5 all-reduce.3
  1326.1 485.2 all-reduce.7
  1814.3 42.2 all-reduce.5
